TPU v7x, 32 devices: a whole 2x2x4 slice. The times are simulated.
32 devices in a mesh: rep: 4 (over z), fsdp: 2 (over x), seq: 4 (over y, core).
Axes of the slice: x: 2, y: 2, z: 4, core: 2. Of those that a mesh axis runs over, the one named last changes fastest.
Arguments:
- tokens: bfloat16 [8, 1024, 640], P(('rep', 'fsdp'), 'seq'), may hold values from -6 to 6
- d_out: bfloat16 [8, 1024, 640], P(('rep', 'fsdp'), 'seq'), may hold values from -6 to 6
- doc_lengths: int32 [8, 3], P(('rep', 'fsdp')), may hold values from 1 to 640, 1024 in all within a row
- w_query: bfloat16 [640, 1024], P('fsdp'), may hold values from -0.25 to 0.25
- w_key: bfloat16 [640, 256], P('fsdp'), may hold values from -0.25 to 0.25
- w_value: bfloat16 [640, 256], P('fsdp'), may hold values from -0.25 to 0.25
- w_out: bfloat16 [1024, 640], P('fsdp'), may hold values from -0.1875 to 0.1875
- w_gate: bfloat16 [640, 2048], P('fsdp'), may hold values from -0.25 to 0.25
- w_up: bfloat16 [640, 2048], P('fsdp'), may hold values from -0.25 to 0.25
- w_down: bfloat16 [2048, 640], P('fsdp'), may hold values from -0.125 to 0.125
- g_input: bfloat16 [640], P('fsdp'), may hold values from 0.5 to 1.5
- g_query: bfloat16 [256], P('fsdp'), may hold values from 0.25 to 1.75
- g_key: bfloat16 [256], P('fsdp'), may hold values from 0.25 to 1.75
- g_attn: bfloat16 [640], P('fsdp'), may hold values from 0.5 to 1.5
- g_ffin: bfloat16 [640], P('fsdp'), may hold values from 0.5 to 1.5
- g_ffout: bfloat16 [640], P('fsdp'), may hold values from 0.5 to 1.5
Outputs:
- result: bfloat16 [8, 1024, 640], P(('rep', 'fsdp'), 'seq')
- d_tokens: bfloat16 [8, 1024, 640], P(('rep', 'fsdp'), 'seq')
- grad_query: float32 [640, 1024], P('fsdp')
- grad_key: float32 [640, 256], P('fsdp')
- grad_value: float32 [640, 256], P('fsdp')
- grad_out: float32 [1024, 640], P('fsdp')
- grad_gate: float32 [640, 2048], P('fsdp')
- grad_up: float32 [640, 2048], P('fsdp')
- grad_down: float32 [2048, 640], P('fsdp')
- grad_ginput: float32 [640], P('fsdp')
- grad_gquery: float32 [256], P('fsdp')
- grad_gkey: float32 [256], P('fsdp')
- grad_gattn: float32 [640], P('fsdp')
- grad_gffin: float32 [640], P('fsdp')
- grad_gffout: float32 [640], P('fsdp')
Inputs may be any that keep to these rules, and one draw needn't show every extreme that they name: `doc_lengths`: each row lists the lengths of the 3 documents packed in order into one sequence; a row sums to 1024 and its largest entry is 640.
All inputs are finite; a program needn't handle non-finite values.
Results may differ from a plain program's by a relative error of at most 0.024.
Values may be sent and summed in bfloat16 or wider, within the bound.
A program may use at most 128 MiB of HBM per device.

v0:
```python
import jax
import jax.numpy as jnp
from jax import lax
from jax.sharding import PartitionSpec as P

EPS = 1e-06
ROPE_BASE = 1000000.0
MASKED = -1e30


def rms_norm(values, gain_vec):
    return values * lax.rsqrt(jnp.mean(values * values, axis=-1, keepdims=True) + EPS) * gain_vec


def rotate(values, angles):
    half_width = values.shape[-1] // 2
    front_half = values[..., :half_width]
    back_half = values[..., half_width:]
    cos_part = jnp.cos(angles)
    sin_part = jnp.sin(angles)
    return jnp.concatenate(
        [
            front_half * cos_part - back_half * sin_part,
            back_half * cos_part + front_half * sin_part,
        ],
        axis=-1,
    )


def frequencies(head_size):
    return jnp.power(
        jnp.float32(ROPE_BASE), -2.0 * jnp.arange(head_size // 2, dtype=jnp.float32) / head_size
    )


def layout(lengths_row, total_len):
    doc_ends = jnp.cumsum(lengths_row)
    starts = doc_ends - lengths_row
    indices = jnp.arange(total_len, dtype=jnp.int32)
    segment = jnp.sum((indices[:, None] >= doc_ends[None, :]).astype(jnp.int32), axis=1)
    onehot = segment[:, None] == jnp.arange(lengths_row.shape[0], dtype=jnp.int32)[None, :]
    doc_begin = jnp.sum(jnp.where(onehot, starts[None, :], 0), axis=1)
    return (segment, indices - doc_begin)


def matmul(left_side, right_side):
    return jnp.dot(left_side, right_side, preferred_element_type=jnp.float32)


def times_transpose(left_side, right_side):
    return lax.dot_general(
        left_side, right_side, (((1,), (1,)), ((), ())), preferred_element_type=jnp.float32
    )


def transpose_times(left_side, right_side):
    return lax.dot_general(
        left_side, right_side, (((0,), (0,)), ((), ())), preferred_element_type=jnp.float32
    )


def gated(gate_proj, up_proj):
    return jax.nn.gelu(gate_proj, approximate=True) * up_proj


def body(
    tokens,
    d_out,
    doc_lengths,
    w_query,
    w_key,
    w_value,
    w_out,
    w_gate,
    w_up,
    w_down,
    g_input,
    g_query,
    g_key,
    g_attn,
    g_ffin,
    g_ffout,
):
    gathered = (
        lax.all_gather(w_query, "fsdp", axis=0, tiled=True),
        lax.all_gather(w_key, "fsdp", axis=0, tiled=True),
        lax.all_gather(w_value, "fsdp", axis=0, tiled=True),
        lax.all_gather(w_out, "fsdp", axis=0, tiled=True),
        lax.all_gather(w_gate, "fsdp", axis=0, tiled=True),
        lax.all_gather(w_up, "fsdp", axis=0, tiled=True),
        lax.all_gather(w_down, "fsdp", axis=0, tiled=True),
        lax.all_gather(g_input, "fsdp", axis=0, tiled=True),
        lax.all_gather(g_query, "fsdp", axis=0, tiled=True),
        lax.all_gather(g_key, "fsdp", axis=0, tiled=True),
        lax.all_gather(g_attn, "fsdp", axis=0, tiled=True),
        lax.all_gather(g_ffin, "fsdp", axis=0, tiled=True),
        lax.all_gather(g_ffout, "fsdp", axis=0, tiled=True),
    )
    query_mat, key_mat, value_mat, out_mat, gate_mat, up_mat, down_mat = gathered[:7]
    gain_input, gain_query, gain_key, gain_attn, gain_ffin, gain_ffout = [
        entry.astype(jnp.float32) for entry in gathered[7:]
    ]
    row_count = tokens.shape[1]
    head_size = gain_query.shape[0]
    head_count = query_mat.shape[1] // head_size
    total_len = row_count * lax.axis_size("seq")
    segment, position = layout(doc_lengths[0], total_len)
    offset = lax.axis_index("seq") * row_count
    query_seg = lax.dynamic_slice_in_dim(segment, offset, row_count)
    query_pos = lax.dynamic_slice_in_dim(position, offset, row_count)
    places = offset + jnp.arange(row_count, dtype=jnp.int32)
    allowed = (query_seg[:, None] == segment[None, :]) & (
        places[:, None] >= jnp.arange(total_len, dtype=jnp.int32)[None, :]
    )
    angles = query_pos.astype(jnp.float32)[:, None] * frequencies(head_size)[None, :]
    scaling = head_size ** (-0.5)
    inputs = tokens[0].astype(jnp.float32)
    cotangent = d_out[0].astype(jnp.float32)
    input_norm, input_pull = jax.vjp(rms_norm, inputs, gain_input)
    attn_input = input_norm.astype(jnp.bfloat16)
    q_proj = matmul(attn_input, query_mat)
    k_proj = matmul(attn_input, key_mat)
    v_proj = matmul(attn_input, value_mat)

    def query_fn(projected, gain_vec):
        shaped = projected.reshape(projected.shape[0], -1, gain_vec.shape[0])
        return rotate(rms_norm(shaped, gain_vec), angles[:, None, :])

    def key_fn(projected, gain_vec):
        return rotate(rms_norm(projected, gain_vec), angles)

    queries, query_pull = jax.vjp(query_fn, q_proj, gain_query)
    keys_own, key_pull = jax.vjp(key_fn, k_proj, gain_key)
    query_rows = queries.astype(jnp.bfloat16).reshape(row_count * head_count, head_size)
    key_rows, value_rows = (
        lax.all_gather(keys_own.astype(jnp.bfloat16), "seq", axis=0, tiled=True),
        lax.all_gather(v_proj.astype(jnp.bfloat16), "seq", axis=0, tiled=True),
    )

    def masked_scores():
        raw_scores = times_transpose(query_rows, key_rows).reshape(row_count, head_count, total_len)
        return jnp.where(allowed[:, None, :], raw_scores * scaling, MASKED)

    scores = masked_scores()
    top_score = jnp.max(scores, axis=-1, keepdims=True)
    shifted = jnp.exp(scores - top_score)
    denominator = jnp.sum(shifted, axis=-1, keepdims=True)
    log_total = top_score + jnp.log(denominator)
    probs_low = (
        (shifted / denominator).astype(jnp.bfloat16).reshape(row_count * head_count, total_len)
    )
    mixed_rows = (
        matmul(probs_low, value_rows)
        .reshape(row_count, head_count * head_size)
        .astype(jnp.bfloat16)
    )
    out_proj = matmul(mixed_rows, out_mat)
    attn_norm, attn_pull = jax.vjp(rms_norm, out_proj, gain_attn)
    hidden_one = inputs + attn_norm
    ffin_norm, ffin_pull = jax.vjp(rms_norm, hidden_one, gain_ffin)
    ff_input = ffin_norm.astype(jnp.bfloat16)
    gate_proj = matmul(ff_input, gate_mat)
    up_proj = matmul(ff_input, up_mat)
    activated, gated_pull = jax.vjp(gated, gate_proj, up_proj)
    hidden = activated.astype(jnp.bfloat16)
    down_proj = matmul(hidden, down_mat)
    ffout_norm, ffout_pull = jax.vjp(rms_norm, down_proj, gain_ffout)
    result = hidden_one + ffout_norm
    query_mat, key_mat, value_mat, out_mat, gate_mat, up_mat, down_mat = (
        lax.all_gather(w_query, "fsdp", axis=0, tiled=True),
        lax.all_gather(w_key, "fsdp", axis=0, tiled=True),
        lax.all_gather(w_value, "fsdp", axis=0, tiled=True),
        lax.all_gather(w_out, "fsdp", axis=0, tiled=True),
        lax.all_gather(w_gate, "fsdp", axis=0, tiled=True),
        lax.all_gather(w_up, "fsdp", axis=0, tiled=True),
        lax.all_gather(w_down, "fsdp", axis=0, tiled=True),
    )
    d_down, grad_gffout = ffout_pull(cotangent)
    d_down_low = d_down.astype(jnp.bfloat16)
    grad_down = transpose_times(hidden, d_down_low)
    d_hidden = times_transpose(d_down_low, down_mat)
    d_gate, d_up = gated_pull(d_hidden)
    d_gate_low = d_gate.astype(jnp.bfloat16)
    d_up_low = d_up.astype(jnp.bfloat16)
    grad_gate = transpose_times(ff_input, d_gate_low)
    grad_up = transpose_times(ff_input, d_up_low)
    d_ffin = times_transpose(d_gate_low, gate_mat) + times_transpose(d_up_low, up_mat)
    d_hidden_part, grad_gffin = ffin_pull(d_ffin)
    d_hidden_one = cotangent + d_hidden_part
    d_out_proj, grad_gattn = attn_pull(d_hidden_one)
    d_out_low = d_out_proj.astype(jnp.bfloat16)
    grad_out = transpose_times(mixed_rows, d_out_low)
    d_mixed = (
        times_transpose(d_out_low, out_mat)
        .astype(jnp.bfloat16)
        .reshape(row_count * head_count, head_size)
    )
    probs_full = jnp.exp(masked_scores() - log_total)
    d_probs = times_transpose(d_mixed, value_rows).reshape(row_count, head_count, total_len)
    row_dot = jnp.sum(probs_full * d_probs, axis=-1, keepdims=True)
    d_raw = (
        (probs_full * (d_probs - row_dot) * scaling)
        .astype(jnp.bfloat16)
        .reshape(row_count * head_count, total_len)
    )
    d_queries = matmul(d_raw, key_rows).reshape(row_count, head_count, head_size)
    grad_key_rows = transpose_times(d_raw, query_rows)
    grad_value_rows = transpose_times(probs_low, d_mixed)
    d_keys_own, d_values_own = (
        lax.psum_scatter(
            grad_key_rows.astype(jnp.bfloat16), "seq", scatter_dimension=0, tiled=True
        ).astype(jnp.float32),
        lax.psum_scatter(
            grad_value_rows.astype(jnp.bfloat16), "seq", scatter_dimension=0, tiled=True
        ).astype(jnp.float32),
    )
    d_q_proj, grad_gquery = query_pull(d_queries)
    d_k_proj, grad_gkey = key_pull(d_keys_own)
    d_q_low = d_q_proj.astype(jnp.bfloat16)
    d_k_low = d_k_proj.astype(jnp.bfloat16)
    d_v_low = d_values_own.astype(jnp.bfloat16)
    grad_query = transpose_times(attn_input, d_q_low)
    grad_key = transpose_times(attn_input, d_k_low)
    grad_value = transpose_times(attn_input, d_v_low)
    d_attn_input = (
        times_transpose(d_q_low, query_mat)
        + times_transpose(d_k_low, key_mat)
        + times_transpose(d_v_low, value_mat)
    )
    d_inputs_part, grad_ginput = input_pull(d_attn_input)
    d_inputs = d_hidden_one + d_inputs_part
    shards = (
        lax.psum_scatter(
            grad_query.astype(jnp.bfloat16), "fsdp", scatter_dimension=0, tiled=True
        ).astype(jnp.float32),
        lax.psum_scatter(
            grad_key.astype(jnp.bfloat16), "fsdp", scatter_dimension=0, tiled=True
        ).astype(jnp.float32),
        lax.psum_scatter(
            grad_value.astype(jnp.bfloat16), "fsdp", scatter_dimension=0, tiled=True
        ).astype(jnp.float32),
        lax.psum_scatter(
            grad_out.astype(jnp.bfloat16), "fsdp", scatter_dimension=0, tiled=True
        ).astype(jnp.float32),
        lax.psum_scatter(
            grad_gate.astype(jnp.bfloat16), "fsdp", scatter_dimension=0, tiled=True
        ).astype(jnp.float32),
        lax.psum_scatter(
            grad_up.astype(jnp.bfloat16), "fsdp", scatter_dimension=0, tiled=True
        ).astype(jnp.float32),
        lax.psum_scatter(
            grad_down.astype(jnp.bfloat16), "fsdp", scatter_dimension=0, tiled=True
        ).astype(jnp.float32),
        lax.psum_scatter(
            grad_ginput.astype(jnp.bfloat16), "fsdp", scatter_dimension=0, tiled=True
        ).astype(jnp.float32),
        lax.psum_scatter(
            grad_gquery.astype(jnp.bfloat16), "fsdp", scatter_dimension=0, tiled=True
        ).astype(jnp.float32),
        lax.psum_scatter(
            grad_gkey.astype(jnp.bfloat16), "fsdp", scatter_dimension=0, tiled=True
        ).astype(jnp.float32),
        lax.psum_scatter(
            grad_gattn.astype(jnp.bfloat16), "fsdp", scatter_dimension=0, tiled=True
        ).astype(jnp.float32),
        lax.psum_scatter(
            grad_gffin.astype(jnp.bfloat16), "fsdp", scatter_dimension=0, tiled=True
        ).astype(jnp.float32),
        lax.psum_scatter(
            grad_gffout.astype(jnp.bfloat16), "fsdp", scatter_dimension=0, tiled=True
        ).astype(jnp.float32),
    )
    totals = (
        lax.psum(shards[0].astype(jnp.bfloat16), ("rep", "seq")).astype(jnp.float32),
        lax.psum(shards[1].astype(jnp.bfloat16), ("rep", "seq")).astype(jnp.float32),
        lax.psum(shards[2].astype(jnp.bfloat16), ("rep", "seq")).astype(jnp.float32),
        lax.psum(shards[3].astype(jnp.bfloat16), ("rep", "seq")).astype(jnp.float32),
        lax.psum(shards[4].astype(jnp.bfloat16), ("rep", "seq")).astype(jnp.float32),
        lax.psum(shards[5].astype(jnp.bfloat16), ("rep", "seq")).astype(jnp.float32),
        lax.psum(shards[6].astype(jnp.bfloat16), ("rep", "seq")).astype(jnp.float32),
        lax.psum(shards[7].astype(jnp.bfloat16), ("rep", "seq")).astype(jnp.float32),
        lax.psum(shards[8].astype(jnp.bfloat16), ("rep", "seq")).astype(jnp.float32),
        lax.psum(shards[9].astype(jnp.bfloat16), ("rep", "seq")).astype(jnp.float32),
        lax.psum(shards[10].astype(jnp.bfloat16), ("rep", "seq")).astype(jnp.float32),
        lax.psum(shards[11].astype(jnp.bfloat16), ("rep", "seq")).astype(jnp.float32),
        lax.psum(shards[12].astype(jnp.bfloat16), ("rep", "seq")).astype(jnp.float32),
    )
    return (
        result.astype(jnp.bfloat16)[None],
        d_inputs.astype(jnp.bfloat16)[None],
        totals[0],
        totals[1],
        totals[2],
        totals[3],
        totals[4],
        totals[5],
        totals[6],
        totals[7],
        totals[8],
        totals[9],
        totals[10],
        totals[11],
        totals[12],
    )


def solution(mesh):
    in_specs = (
        P(("rep", "fsdp"), "seq", None),
        P(("rep", "fsdp"), "seq", None),
        P(("rep", "fsdp"), None),
        P("fsdp", None),
        P("fsdp", None),
        P("fsdp", None),
        P("fsdp", None),
        P("fsdp", None),
        P("fsdp", None),
        P("fsdp", None),
        P("fsdp"),
        P("fsdp"),
        P("fsdp"),
        P("fsdp"),
        P("fsdp"),
        P("fsdp"),
    )
    out_specs = (
        P(("rep", "fsdp"), "seq", None),
        P(("rep", "fsdp"), "seq", None),
        P("fsdp", None),
        P("fsdp", None),
        P("fsdp", None),
        P("fsdp", None),
        P("fsdp", None),
        P("fsdp", None),
        P("fsdp", None),
        P("fsdp"),
        P("fsdp"),
        P("fsdp"),
        P("fsdp"),
        P("fsdp"),
        P("fsdp"),
    )
    return jax.shard_map(body, mesh=mesh, in_specs=in_specs, out_specs=out_specs, check_vma=False)
```

profile of v0, /device:TPU:0, one launch (start us, length us, event | category | flops | bytes accessed | tf_op | source)
XLA Modules:
  0.0 610.9 jit_solution(18083511794878233762)
XLA Ops:
  11.2 5.2 all-gather
  16.3 4.2 all-gather.1
  22.8 5.3 all-reduce.17
  29.0 10.0 %all_gather.55 = bf16[640,256]{1,0:T(8,128)(2,1)S(1)} all-gather(bf16[320,256]{1,0:T(8,128)(2,1)S(1)} %copy-done.38), channel_id=1, replica_groups=mesh['rep'=4,'fsdp'=2,'seq'=4] {'fsdp'}, dimensions={0}, use_global_device_ids=true | all-gather | bytes 491520 | tf_op jit(solution)/shard_map/all_gather | solution.py:86
  39.5 6.0 all_gather.58
  45.8 8.1 %all_gather.59 = bf16[1024,256]{1,0:T(8,128)(2,1)} all-gather(bf16[256,256]{1,0:T(8,128)(2,1)S(1)} %convolution_convert_fusion.10), channel_id=1, replica_groups=mesh['rep'=4,'fsdp'=2,'seq'=4] {'seq'}, dimensions={0}, use_global_device_ids=true | all-gather | bytes 655360 | tf_op jit(solution)/shard_map/all_gather | solution.py:137
  54.7 7.3 %all_gather.57 = bf16[1024,256]{0,1:T(8,128)(2,1)S(1)} all-gather(bf16[256,256]{0,1:T(8,128)(2,1)S(1)} %pad_maximum_fusion.3), channel_id=1, replica_groups=mesh['rep'=4,'fsdp'=2,'seq'=4] {'seq'}, dimensions={0}, use_global_device_ids=true | all-gather | bytes 655360 | tf_op jit(solution)/shard_map/all_gather | solution.py:136
  63.1 1.7 copy.54
  70.2 1.6 copy.57
  71.9 2.0 reshape.332
  73.9 2.7 convolution_convert_fusion.7
  76.9 2.1 multiply_reduce_fusion.10
  80.6 26.2 %all-gather.12.cloned.1.call-done = bf16[640,2048]{1,0:T(8,128)(2,1)} async-done(((bf16[320,2048]{1,0:T(8,128)(2,1)}), bf16[640,2048]{1,0:T(8,128)(2,1)}) %all-gather.12.cloned.1.call-update) | async-done | bytes 2621456 | tf_op jit(solution)/shard_map/all_gather | solution.py:89
  106.9 4.0 fusion.103
  110.9 36.4 %all-gather.14.cloned.1.call-done = bf16[640,2048]{1,0:T(8,128)(2,1)} async-done(((bf16[320,2048]{1,0:T(8,128)(2,1)}), bf16[640,2048]{1,0:T(8,128)(2,1)}) %all-gather.14.cloned.1.call-update) | async-done | bytes 2621456 | tf_op jit(solution)/shard_map/all_gather | solution.py:90
  147.3 5.2 multiply_convert_fusion.2
  152.6 35.2 %all-gather.16.cloned.1.call-done = bf16[2048,640]{1,0:T(8,128)(2,1)} async-done(((bf16[1024,640]{1,0:T(8,128)(2,1)}), bf16[2048,640]{1,0:T(8,128)(2,1)}) %all-gather.16.cloned.1.call-update) | async-done | bytes 2621456 | tf_op jit(solution)/shard_map/all_gather | solution.py:91
  187.7 3.3 multiply_reduce_fusion.8
  192.9 2.5 multiply_convert_fusion.1
  196.7 1.2 copy-done.10
  197.9 1.7 multiply_reduce_fusion.4
  203.3 3.2 convolution_convert_fusion.5
  206.6 3.9 fusion.54
  210.5 12.4 %fusion.27 = bf16[1024,256]{0,1:T(8,128)(2,1)} fusion(f32[256,4,1024]{2,0,1:T(8,128)} %fusion.54, f32[256,4,1024]{2,0,1:T(8,128)} %copy-done, f32[256,4]{0,1:T(4,128)S(1)} %log_add_fusion, bf16[256,4,128]{0,2,1:T(8,128)(2,1)} %copy-done.36, bf16[256,4,128]{0,2,1:T(8,128)(2,1)S(1)} %copy-done.35), kind=kOutput, calls=%fused_computation.34 | convolution fusion | flops 545523712 | bytes 9441280 | tf_op jit(solution)/shard_map/dot_general | solution.py:57
  223.0 5.3 reduce-scatter.12.cloned.1.call-done
  228.4 2.0 convolution_convert_fusion.8
  230.5 22.6 %reduce-scatter.10.cloned.1.call-done = bf16[256,256]{0,1:T(8,128)(2,1)} async-done(((bf16[1024,256]{0,1:T(8,128)(2,1)}), bf16[256,256]{0,1:T(8,128)(2,1)}) %reduce-scatter.10.cloned.1.call-update) | async-done | bytes 131088 | tf_op jit(solution)/shard_map/reduce_scatter | solution.py:210
  256.2 1.7 convolution_convert_fusion.3
  257.9 10.5 %fusion.9 = f32[256,4,256]{0,2,1:T(8,128)S(1)} fusion(f32[256,4,1024]{2,0,1:T(8,128)} %fusion.54, f32[256,4,1024]{2,0,1:T(8,128)} %copy-done, f32[256,4]{0,1:T(4,128)S(1)} %log_add_fusion, bf16[1024,256]{0,1:T(8,128)(2,1)} %copy-done.33), kind=kOutput, calls=%fused_computation.15 | convolution fusion | flops 544212992 | bytes 9965568 | tf_op jit(solution)/shard_map/dot_general | solution.py:47
  270.2 1.7 convolution_convert_fusion.4
  272.0 2.4 convolution_convert_fusion.1
  275.6 2.4 convolution_convert_fusion.2
  279.3 2.5 convolution_convert_fusion
  281.9 1.3 reduce-scatter.16.cloned.1.call-done
  283.2 26.0 %reduce-scatter.20.cloned.1.call-done = bf16[512,640]{1,0:T(8,128)(2,1)} async-done(((bf16[1024,640]{1,0:T(8,128)(2,1)}), bf16[512,640]{1,0:T(8,128)(2,1)}) %reduce-scatter.20.cloned.1.call-update) | async-done | bytes 655376 | tf_op jit(solution)/shard_map/reduce_scatter | solution.py:242
  309.2 26.1 %reduce-scatter.14.cloned.1.call-done = bf16[320,1024]{1,0:T(8,128)(2,1)} async-done(((bf16[640,1024]{1,0:T(8,128)(2,1)}), bf16[320,1024]{1,0:T(8,128)(2,1)}) %reduce-scatter.14.cloned.1.call-update) | async-done | bytes 655376 | tf_op jit(solution)/shard_map/reduce_scatter | solution.py:233
  335.3 40.4 %reduce-scatter.24.cloned.1.call-done = bf16[320,2048]{1,0:T(8,128)(2,1)} async-done(((bf16[640,2048]{1,0:T(8,128)(2,1)}), bf16[320,2048]{1,0:T(8,128)(2,1)}) %reduce-scatter.24.cloned.1.call-update) | async-done | bytes 1310736 | tf_op jit(solution)/shard_map/reduce_scatter | solution.py:248
  375.7 40.5 %reduce-scatter.22.cloned.1.call-done = bf16[320,2048]{1,0:T(8,128)(2,1)} async-done(((bf16[640,2048]{1,0:T(8,128)(2,1)}), bf16[320,2048]{1,0:T(8,128)(2,1)}) %reduce-scatter.22.cloned.1.call-update) | async-done | bytes 1310736 | tf_op jit(solution)/shard_map/reduce_scatter | solution.py:245
  416.2 40.4 %reduce-scatter.26.cloned.1.call-done = bf16[1024,640]{1,0:T(8,128)(2,1)} async-done(((bf16[2048,640]{1,0:T(8,128)(2,1)}), bf16[1024,640]{1,0:T(8,128)(2,1)}) %reduce-scatter.26.cloned.1.call-update) | async-done | bytes 1310736 | tf_op jit(solution)/shard_map/reduce_scatter | solution.py:251
  459.6 5.1 all-reduce.16
  465.1 34.6 %all-reduce.14 = (bf16[320]{0:T(512)(128)(2,1)S(1)}, bf16[128]{0:T(256)(128)(2,1)S(1)}, bf16[128]{0:T(256)(128)(2,1)S(1)}, bf16[320]{0:T(512)(128)(2,1)S(1)}, bf...) all-reduce(bf16[320]{0:T(512)(128)(2,1)S(1)} %dynamic-slice.5, ...), channel_id=1, replica_groups=mesh['rep'=4,'fsdp'=2,'seq'=4] {'rep','seq'}, use_global_device_ids=true, to_apply=%region_36.37 | all-reduce | flops 1536 | bytes 6144 | tf_op jit(solution)/shard_map/psum | solution.py:281
  504.0 88.2 %all-reduce.20.cloned.1.call-done = (bf16[320,1024]{1,0:T(8,128)(2,1)}, bf16[320,256]{1,0:T(8,128)(2,1)}, bf16[320,256]{1,0:T(8,128)(2,1)}, bf16[512,640]{1,0:T(...) async-done(((bf16[320,1024]{1,0:T(8,128)(2,1)}, bf16[320,256]{1,0:T(8,128)(2,1)}, bf16[320,256]{1,0:T(8,128)(2,1)}, ...) | async-done | bytes 5570576 | tf_op jit(solution)/shard_map/psum | solution.py:274
  592.2 1.7 convert_element_type.259
  593.9 1.8 convert_element_type.261
  595.7 2.3 convert_element_type.257
  599.2 1.8 convert_element_type.265
  601.0 1.8 convert_element_type.267
  602.8 1.7 convert_element_type.269
  (289 shorter events, 37.6 us)
Async XLA Ops:
  7.2 55.9 %all-gather.8.cloned.1.call-start = ((), (), s32[]{:S(2)}) async-start(), calls=%async_computation.9 | async-start | bytes 1966080 | tf_op jit(solution)/shard_map/all_gather | solution.py:85
  7.9 69.0 %all-gather.10.cloned.1.call-start = ((), (), s32[]{:S(2)}) async-start(), calls=%async_computation.10 | async-start | bytes 1966080 | tf_op jit(solution)/shard_map/all_gather | solution.py:88
  8.7 7.6 %copy-start.84 = (bf16[128]{0:T(256)(128)(2,1)S(1)}, bf16[128]{0:T(256)(128)(2,1)}, u32[]{:S(2)}) copy-start(bf16[128]{0:T(256)(128)(2,1)} %param.28) | copy-start | bytes 772
  8.7 11.9 %copy-start.74 = (u32[32]{0:T(128)S(1)}, u32[32]{0:T(128)}, u32[]{:S(2)}) copy-start(u32[32]{0:T(128)} %constant.76) | copy-start | bytes 388
  8.7 13.1 %copy-start.77 = (bf16[320]{0:T(512)(128)(2,1)S(1)}, bf16[320]{0:T(512)(128)(2,1)}, u32[]{:S(2)}) copy-start(bf16[320]{0:T(512)(128)(2,1)} %param.30) | copy-start | bytes 1924
  8.7 13.4 %copy-start.78 = (bf16[320]{0:T(512)(128)(2,1)S(1)}, bf16[320]{0:T(512)(128)(2,1)}, u32[]{:S(2)}) copy-start(bf16[320]{0:T(512)(128)(2,1)} %param.29) | copy-start | bytes 1924
  8.7 13.6 %copy-start.79 = (bf16[320]{0:T(512)(128)(2,1)S(1)}, bf16[320]{0:T(512)(128)(2,1)}, u32[]{:S(2)}) copy-start(bf16[320]{0:T(512)(128)(2,1)} %param.26) | copy-start | bytes 1924
  8.7 13.8 %copy-start.80 = (bf16[320]{0:T(512)(128)(2,1)S(1)}, bf16[320]{0:T(512)(128)(2,1)}, u32[]{:S(2)}) copy-start(bf16[320]{0:T(512)(128)(2,1)} %param.31) | copy-start | bytes 1924
  8.8 20.3 %copy-start.38 = (bf16[320,256]{1,0:T(8,128)(2,1)S(1)}, bf16[320,256]{1,0:T(8,128)(2,1)}, u32[]{:S(2)}) copy-start(bf16[320,256]{1,0:T(8,128)(2,1)} %param.20) | copy-start | bytes 491524
  8.8 98.1 %all-gather.12.cloned.1.call-start = ((), (), s32[]{:S(2)}) async-start(), calls=%async_computation.11 | async-start | bytes 3932160 | tf_op jit(solution)/shard_map/all_gather | solution.py:89
  9.5 30.0 %copy-start.39 = (bf16[320,256]{1,0:T(8,128)(2,1)S(1)}, bf16[320,256]{1,0:T(8,128)(2,1)}, u32[]{:S(2)}) copy-start(bf16[320,256]{1,0:T(8,128)(2,1)} %param.21) | copy-start | bytes 491524
  9.5 137.8 %all-gather.14.cloned.1.call-start = ((), (), s32[]{:S(2)}) async-start(), calls=%async_computation.12 | async-start | bytes 3932160 | tf_op jit(solution)/shard_map/all_gather | solution.py:90
  10.1 177.6 %all-gather.16.cloned.1.call-start = ((), (), s32[]{:S(2)}) async-start(), calls=%async_computation.13 | async-start | bytes 3932160 | tf_op jit(solution)/shard_map/all_gather | solution.py:91
  10.7 217.7 %reduce-scatter.12.cloned.1.call-start = ((), (), s32[]{:S(2)}) async-start(), calls=%async_computation.15 | async-start | bytes 655360 | tf_op jit(solution)/shard_map/reduce_scatter | solution.py:213
  10.8 43.3 %copy-start.75 = (f32[128]{0:T(128)}, f32[128]{0:T(128)S(1)}, u32[]{:S(2)}) copy-start(f32[128]{0:T(128)S(1)} %multiply_power_fusion) | copy-start | bytes 1540
  11.1 42.9 %copy-start.62 = (f32[256]{0:T(256)}, f32[256]{0:T(256)S(1)}, u32[]{:S(2)}) copy-start(f32[256]{0:T(256)S(1)} %fusion.45) | copy-start | bytes 3076
  11.1 53.7 %copy-start.48 = (f32[256]{0:T(256)}, f32[256]{0:T(256)S(1)}, u32[]{:S(2)}) copy-start(f32[256]{0:T(256)S(1)} %fusion.83) | copy-start | bytes 3076
  16.3 49.2 %copy-start.52 = (f32[2,1,128]{2,1,0:T(1,128)}, f32[2,1,128]{2,1,0:T(1,128)S(1)}, u32[]{:S(2)}) copy-start(f32[2,1,128]{2,1,0:T(1,128)S(1)} %convert_element_type.284) | copy-start | bytes 3076
  20.6 33.5 %copy-start.54 = (f32[2,1,128]{2,1,0:T(1,128)}, f32[2,1,128]{2,1,0:T(1,128)S(1)}, u32[]{:S(2)}) copy-start(f32[2,1,128]{2,1,0:T(1,128)S(1)} %convert_element_type.285) | copy-start | bytes 3076
  28.4 26.2 %copy-start.60 = (f32[256]{0:T(256)}, f32[256]{0:T(256)S(1)}, u32[]{:S(2)}) copy-start(f32[256]{0:T(256)S(1)} %dynamic-slice_convert_fusion) | copy-start | bytes 3076
  39.0 15.6 %copy-start.17 = (bf16[640,256]{1,0:T(8,128)(2,1)}, bf16[640,256]{1,0:T(8,128)(2,1)S(1)}, u32[]{:S(2)}) copy-start(bf16[640,256]{1,0:T(8,128)(2,1)S(1)} %all_gather.55) | copy-start | bytes 983044
  39.4 22.6 %copy-start.11 = (f32[256,256]{0,1:T(8,128)}, f32[256,256]{0,1:T(8,128)S(1)}, u32[]{:S(2)}) copy-start(f32[256,256]{0,1:T(8,128)S(1)} %get-tuple-element.72) | copy-start | bytes 786436
  39.4 22.6 %copy-start.71 = (f32[256]{0:T(256)}, f32[256]{0:T(256)S(1)}, u32[]{:S(2)}) copy-start(f32[256]{0:T(256)S(1)} %get-tuple-element.71) | copy-start | bytes 3076
  39.5 22.5 %copy-start.56 = (f32[256]{0:T(256)}, f32[256]{0:T(256)S(1)}, u32[]{:S(2)}) copy-start(f32[256]{0:T(256)S(1)} %fusion.84) | copy-start | bytes 3076
  45.5 9.2 %copy-start.19 = (bf16[640,256]{1,0:T(8,128)(2,1)}, bf16[640,256]{1,0:T(8,128)(2,1)S(1)}, u32[]{:S(2)}) copy-start(bf16[640,256]{1,0:T(8,128)(2,1)S(1)} %all_gather.58) | copy-start | bytes 983044
  54.7 11.1 %copy-start.23 = (f32[256,128]{0,1:T(8,128)}, f32[256,128]{0,1:T(8,128)S(1)}, u32[]{:S(2)}) copy-start(f32[256,128]{0,1:T(8,128)S(1)} %get-tuple-element.65) | copy-start | bytes 393220
  54.7 11.1 %copy-start.25 = (f32[256,128]{0,1:T(8,128)}, f32[256,128]{0,1:T(8,128)S(1)}, u32[]{:S(2)}) copy-start(f32[256,128]{0,1:T(8,128)S(1)} %get-tuple-element.66) | copy-start | bytes 393220
  206.5 46.6 %reduce-scatter.10.cloned.1.call-start = ((), (), s32[]{:S(2)}) async-start(), calls=%async_computation.14 | async-start | bytes 655360 | tf_op jit(solution)/shard_map/reduce_scatter | solution.py:210
  210.5 17.9 %copy-start.49 = (f32[256]{0:T(256)S(1)}, f32[256]{0:T(256)}, u32[]{:S(2)}) copy-start(f32[256]{0:T(256)} %copy-done.48) | copy-start | bytes 3076
  222.9 31.1 %copy-start.61 = (f32[256]{0:T(256)S(1)}, f32[256]{0:T(256)}, u32[]{:S(2)}) copy-start(f32[256]{0:T(256)} %copy-done.60) | copy-start | bytes 3076
  222.9 31.1 %copy-start.76 = (f32[128]{0:T(128)S(1)}, f32[128]{0:T(128)}, u32[]{:S(2)}) copy-start(f32[128]{0:T(128)} %copy-done.75) | copy-start | bytes 1540
  222.9 31.7 %copy-start.12 = (f32[256,256]{0,1:T(8,128)S(1)}, f32[256,256]{0,1:T(8,128)}, u32[]{:S(2)}) copy-start(f32[256,256]{0,1:T(8,128)} %copy-done.11) | copy-start | bytes 786436
  222.9 31.7 %copy-start.55 = (f32[2,1,128]{2,1,0:T(1,128)S(1)}, f32[2,1,128]{2,1,0:T(1,128)}, u32[]{:S(2)}) copy-start(f32[2,1,128]{2,1,0:T(1,128)} %copy-done.54) | copy-start | bytes 3076
  222.9 31.7 %copy-start.57 = (f32[256]{0:T(256)S(1)}, f32[256]{0:T(256)}, u32[]{:S(2)}) copy-start(f32[256]{0:T(256)} %copy-done.56) | copy-start | bytes 3076
  222.9 31.9 %copy-start.72 = (f32[256]{0:T(256)S(1)}, f32[256]{0:T(256)}, u32[]{:S(2)}) copy-start(f32[256]{0:T(256)} %copy-done.71) | copy-start | bytes 3076
  223.0 58.9 %reduce-scatter.18.cloned.1.call-start = ((), (), s32[]{:S(2)}) async-start(), calls=%async_computation.18 | async-start | bytes 491520 | tf_op jit(solution)/shard_map/reduce_scatter | solution.py:239
  230.4 52.8 %reduce-scatter.16.cloned.1.call-start = ((), (), s32[]{:S(2)}) async-start(), calls=%async_computation.17 | async-start | bytes 491520 | tf_op jit(solution)/shard_map/reduce_scatter | solution.py:236
  256.1 53.0 %reduce-scatter.20.cloned.1.call-start = ((), (), s32[]{:S(2)}) async-start(), calls=%async_computation.19 | async-start | bytes 1966080 | tf_op jit(solution)/shard_map/reduce_scatter | solution.py:242
  257.9 10.5 %copy-start.24 = (f32[256,128]{0,1:T(8,128)S(1)}, f32[256,128]{0,1:T(8,128)}, u32[]{:S(2)}) copy-start(f32[256,128]{0,1:T(8,128)} %copy-done.23) | copy-start | bytes 393220
  257.9 10.5 %copy-start.26 = (f32[256,128]{0,1:T(8,128)S(1)}, f32[256,128]{0,1:T(8,128)}, u32[]{:S(2)}) copy-start(f32[256,128]{0,1:T(8,128)} %copy-done.25) | copy-start | bytes 393220
  257.9 77.4 %reduce-scatter.14.cloned.1.call-start = ((), (), s32[]{:S(2)}) async-start(), calls=%async_computation.16 | async-start | bytes 1966080 | tf_op jit(solution)/shard_map/reduce_scatter | solution.py:233
  271.9 103.7 %reduce-scatter.24.cloned.1.call-start = ((), (), s32[]{:S(2)}) async-start(), calls=%async_computation.21 | async-start | bytes 3932160 | tf_op jit(solution)/shard_map/reduce_scatter | solution.py:248
  274.4 141.8 %reduce-scatter.22.cloned.1.call-start = ((), (), s32[]{:S(2)}) async-start(), calls=%async_computation.20 | async-start | bytes 3932160 | tf_op jit(solution)/shard_map/reduce_scatter | solution.py:245
  278.0 178.6 %reduce-scatter.26.cloned.1.call-start = ((), (), s32[]{:S(2)}) async-start(), calls=%async_computation.22 | async-start | bytes 3932160 | tf_op jit(solution)/shard_map/reduce_scatter | solution.py:251
  281.8 310.4 %all-reduce.20.cloned.1.call-start = ((), (), s32[]{:S(2)}) async-start(), calls=%async_computation.23 | async-start | bytes 11141120 | tf_op jit(solution)/shard_map/psum | solution.py:274
  458.8 44.3 %copy-start.63 = (f32[256]{0:T(256)S(1)}, f32[256]{0:T(256)}, u32[]{:S(2)}) copy-start(f32[256]{0:T(256)} %copy-done.62) | copy-start | bytes 3076
  458.8 44.3 %copy-start.3 = (f32[256,640]{1,0:T(8,128)S(1)}, f32[256,640]{1,0:T(8,128)}, u32[]{:S(2)}) copy-start(f32[256,640]{1,0:T(8,128)} %copy-done.2) | copy-start | bytes 1966084
  592.2 5.8 copy-start.30
  (53 other events, 104.1 us)
Sparse Core Ops, SparseCore 0:
  9.5 31.1 all-gather.7
  42.2 24.0 all-gather.9
  67.8 38.9 all-gather.11
  108.3 38.9 all-gather.13
  148.7 38.9 all-gather.15
  206.7 21.6 reduce-scatter.11
  231.4 21.6 reduce-scatter.9
  255.3 12.4 reduce-scatter.17
  270.7 12.4 reduce-scatter.15
  285.8 23.2 reduce-scatter.19
  312.0 23.2 reduce-scatter.13
  338.0 37.6 reduce-scatter.23
  378.5 37.6 reduce-scatter.21
  418.9 37.6 reduce-scatter.25
  461.1 131.0 all-reduce.19
where the time goes:
time: 612 us; the launch traced here: 611 us
  waiting for transfers between devices  392 us (64%)
  blocking collectives  85.7 us (14%)
  matrix products  70.8 us (12%)
  other arithmetic  28 us (5%)
  between operations  17.2 us (3%)
  local copies, waits for them, and re-layouts  16.7 us (3%)
    psum x1, waiting for transfers between devices, body(): lax.psum(shards[0].astype(jnp.bfloat16), ('rep', 'seq')).astype(jnp.float32)  88.2 us
    reduce_scatter x1, waiting for transfers between devices, body(): lax.psum_scatter(grad_gate.astype(jnp.bfloat16), 'fsdp', scatter_dimensio...  40.5 us
    reduce_scatter x1, waiting for transfers between devices, body(): lax.psum_scatter(grad_down.astype(jnp.bfloat16), 'fsdp', scatter_dimensio...  40.4 us
    reduce_scatter x1, waiting for transfers between devices, body(): lax.psum_scatter(grad_up.astype(jnp.bfloat16), 'fsdp', scatter_dimension=...  40.4 us
    all_gather x1, waiting for transfers between devices, body(): lax.all_gather(w_up, 'fsdp', axis=0, tiled=True)  36.4 us
    all_gather x1, waiting for transfers between devices, body(): lax.all_gather(w_down, 'fsdp', axis=0, tiled=True)  35.2 us
    psum x1, blocking collectives, body(): lax.psum(shards[7].astype(jnp.bfloat16), ('rep', 'seq')).astype(jnp.float32)  34.6 us
    dot_general x9, matrix products, transpose_times(): lax.dot_general(left_side, right_side, (((0,), (0,)), ((), ())), preferre...  29.4 us
  transfers between devices with their start and end apart: 15, of which 12 were waited for; matrix products, arithmetic and copies ran while one was open for 13% of the time, Pallas kernels for 0%

commit v1 on v0

--- a/solution.py
+++ b/solution.py
@@ -81,6 +81,12 @@
     g_ffin,
     g_ffout,
 ):
+
+    def map_zone_in(payload):
+        answer = lax.all_gather(payload, axis_name=("rep", "seq"))
+        a_next = jnp.sum(answer, axis=0)
+        return a_next
+
     gathered = (
         lax.all_gather(w_query, "fsdp", axis=0, tiled=True),
         lax.all_gather(w_key, "fsdp", axis=0, tiled=True),
@@ -271,7 +277,7 @@
         ).astype(jnp.float32),
     )
     totals = (
-        lax.psum(shards[0].astype(jnp.bfloat16), ("rep", "seq")).astype(jnp.float32),
+        map_zone_in(shards[0].astype(jnp.bfloat16)).astype(jnp.float32),
         lax.psum(shards[1].astype(jnp.bfloat16), ("rep", "seq")).astype(jnp.float32),
         lax.psum(shards[2].astype(jnp.bfloat16), ("rep", "seq")).astype(jnp.float32),
         lax.psum(shards[3].astype(jnp.bfloat16), ("rep", "seq")).astype(jnp.float32),

time: 612 us -> 691 us (1.13)
  waiting for transfers between devices: 392 us -> 458 us
  other arithmetic: 28 us -> 35.1 us
    all_gather x0 -> x1, waiting for transfers between devices: none -> 78.8 us  [map_zone_in(): answer = lax.all_gather(payload, axis_name=('rep', 'seq'))]
    psum x1, waiting for transfers between devices: 88.2 us -> 76.4 us  [body(): lax.psum(shards[1].astype(jnp.bfloat16), ('rep', 'seq')).astype(jnp.float32)]
  transfers between devices with their start and end apart: 15 -> 16, of which waited for: 12 -> 13; matrix products, arithmetic and copies ran while one was open for 13% -> 13% of each run, Pallas kernels for 0% -> 0%
where the time goes in v1:
time: 691 us; the launch traced here: 687 us
  waiting for transfers between devices  458 us (66%)
  blocking collectives  85.4 us (12%)
  matrix products  71.2 us (10%)
  other arithmetic  35.1 us (5%)
  local copies, waits for them, and re-layouts  18.6 us (3%)
  between operations  17.3 us (3%)
    all_gather x1, waiting for transfers between devices, map_zone_in(): answer = lax.all_gather(payload, axis_name=('rep', 'seq'))  78.8 us
    psum x1, waiting for transfers between devices, body(): lax.psum(shards[1].astype(jnp.bfloat16), ('rep', 'seq')).astype(jnp.float32)  76.4 us
    reduce_scatter x1, waiting for transfers between devices, body(): lax.psum_scatter(grad_up.astype(jnp.bfloat16), 'fsdp', scatter_dimension=...  40.5 us
    reduce_scatter x1, waiting for transfers between devices, body(): lax.psum_scatter(grad_down.astype(jnp.bfloat16), 'fsdp', scatter_dimensio...  40.5 us
    reduce_scatter x1, waiting for transfers between devices, body(): lax.psum_scatter(grad_gate.astype(jnp.bfloat16), 'fsdp', scatter_dimensio...  40.4 us
    all_gather x1, waiting for transfers between devices, body(): lax.all_gather(w_up, 'fsdp', axis=0, tiled=True)  36.4 us
    all_gather x1, waiting for transfers between devices, body(): lax.all_gather(w_down, 'fsdp', axis=0, tiled=True)  35.2 us
    psum x1, blocking collectives, body(): lax.psum(shards[7].astype(jnp.bfloat16), ('rep', 'seq')).astype(jnp.float32)  34.3 us
  transfers between devices with their start and end apart: 16, of which 13 were waited for; matrix products, arithmetic and copies ran while one was open for 13% of the time, Pallas kernels for 0%

profile of v1, /device:TPU:0, one launch (start us, length us, event | category | flops | bytes accessed | tf_op | source)
XLA Modules:
  0.0 686.9 jit_solution(4013533533081355777)
XLA Ops:
  11.2 5.2 all-gather.1
  16.3 4.2 all-gather.2
  22.8 5.3 all-reduce.17
  29.0 10.0 %all_gather.61 = bf16[640,256]{1,0:T(8,128)(2,1)S(1)} all-gather(bf16[320,256]{1,0:T(8,128)(2,1)S(1)} %copy-done.38), channel_id=1, replica_groups=mesh['rep'=4,'fsdp'=2,'seq'=4] {'fsdp'}, dimensions={0}, use_global_device_ids=true | all-gather | bytes 491520 | tf_op jit(solution)/shard_map/all_gather | solution.py:92
  39.5 6.0 all_gather.64
  45.8 8.1 %all_gather.65 = bf16[1024,256]{1,0:T(8,128)(2,1)} all-gather(bf16[256,256]{1,0:T(8,128)(2,1)S(1)} %convolution_convert_fusion.10), channel_id=1, replica_groups=mesh['rep'=4,'fsdp'=2,'seq'=4] {'seq'}, dimensions={0}, use_global_device_ids=true | all-gather | bytes 655360 | tf_op jit(solution)/shard_map/all_gather | solution.py:143
  54.7 7.3 %all_gather.63 = bf16[1024,256]{0,1:T(8,128)(2,1)S(1)} all-gather(bf16[256,256]{0,1:T(8,128)(2,1)S(1)} %pad_maximum_fusion.3), channel_id=1, replica_groups=mesh['rep'=4,'fsdp'=2,'seq'=4] {'seq'}, dimensions={0}, use_global_device_ids=true | all-gather | bytes 655360 | tf_op jit(solution)/shard_map/all_gather | solution.py:142
  63.1 2.1 copy.54
  72.3 2.0 reshape.332
  74.3 2.7 convolution_convert_fusion.7
  77.4 2.1 multiply_reduce_fusion.10
  81.1 25.8 %all-gather.14.cloned.1.call-done = bf16[640,2048]{1,0:T(8,128)(2,1)} async-done(((bf16[320,2048]{1,0:T(8,128)(2,1)}), bf16[640,2048]{1,0:T(8,128)(2,1)}) %all-gather.14.cloned.1.call-update) | async-done | bytes 2621456 | tf_op jit(solution)/shard_map/all_gather | solution.py:95
  106.9 4.0 fusion.103
  110.9 36.4 %all-gather.16.cloned.1.call-done = bf16[640,2048]{1,0:T(8,128)(2,1)} async-done(((bf16[320,2048]{1,0:T(8,128)(2,1)}), bf16[640,2048]{1,0:T(8,128)(2,1)}) %all-gather.16.cloned.1.call-update) | async-done | bytes 2621456 | tf_op jit(solution)/shard_map/all_gather | solution.py:96
  147.3 5.2 multiply_convert_fusion.2
  152.5 35.2 %all-gather.18.cloned.1.call-done = bf16[2048,640]{1,0:T(8,128)(2,1)} async-done(((bf16[1024,640]{1,0:T(8,128)(2,1)}), bf16[2048,640]{1,0:T(8,128)(2,1)}) %all-gather.18.cloned.1.call-update) | async-done | bytes 2621456 | tf_op jit(solution)/shard_map/all_gather | solution.py:97
  187.7 3.3 multiply_reduce_fusion.8
  192.9 2.5 multiply_convert_fusion.1
  197.9 1.7 multiply_reduce_fusion.4
  203.9 3.3 convolution_convert_fusion.5
  207.4 2.8 fusion.54
  210.1 12.4 %fusion.27 = bf16[1024,256]{0,1:T(8,128)(2,1)} fusion(f32[256,4,1024]{2,0,1:T(8,128)} %fusion.54, f32[256,4,1024]{2,0,1:T(8,128)} %copy-done, f32[256,4]{0,1:T(4,128)S(1)} %log_add_fusion, bf16[256,4,128]{0,2,1:T(8,128)(2,1)} %copy-done.36, bf16[256,4,128]{0,2,1:T(8,128)(2,1)S(1)} %copy-done.35), kind=kOutput, calls=%fused_computation.34 | convolution fusion | flops 545523712 | bytes 9441280 | tf_op jit(solution)/shard_map/dot_general | solution.py:57
  222.6 6.5 reduce-scatter.12.cloned.1.call-done
  229.1 2.1 convolution_convert_fusion.8
  231.2 22.6 %reduce-scatter.10.cloned.1.call-done = bf16[256,256]{0,1:T(8,128)(2,1)} async-done(((bf16[1024,256]{0,1:T(8,128)(2,1)}), bf16[256,256]{0,1:T(8,128)(2,1)}) %reduce-scatter.10.cloned.1.call-update) | async-done | bytes 131088 | tf_op jit(solution)/shard_map/reduce_scatter | solution.py:216
  256.9 2.7 convolution_convert_fusion.3
  259.7 2.4 convolution_convert_fusion.1
  263.3 2.4 convolution_convert_fusion.2
  267.0 2.5 convolution_convert_fusion
  270.6 10.1 %fusion.9 = f32[256,4,256]{0,2,1:T(8,128)S(1)} fusion(f32[256,4,1024]{2,0,1:T(8,128)} %fusion.54, f32[256,4,1024]{2,0,1:T(8,128)} %copy-done, f32[256,4]{0,1:T(4,128)S(1)} %log_add_fusion, bf16[1024,256]{0,1:T(8,128)(2,1)S(1)} %copy-done.33), kind=kOutput, calls=%fused_computation.15 | convolution fusion | flops 544212992 | bytes 9965568 | tf_op jit(solution)/shard_map/dot_general | solution.py:47
  282.0 1.7 convolution_convert_fusion.4
  284.0 26.0 %reduce-scatter.20.cloned.1.call-done = bf16[512,640]{1,0:T(8,128)(2,1)} async-done(((bf16[1024,640]{1,0:T(8,128)(2,1)}), bf16[512,640]{1,0:T(8,128)(2,1)}) %reduce-scatter.20.cloned.1.call-update) | async-done | bytes 655376 | tf_op jit(solution)/shard_map/reduce_scatter | solution.py:248
  310.0 40.5 %reduce-scatter.24.cloned.1.call-done = bf16[320,2048]{1,0:T(8,128)(2,1)} async-done(((bf16[640,2048]{1,0:T(8,128)(2,1)}), bf16[320,2048]{1,0:T(8,128)(2,1)}) %reduce-scatter.24.cloned.1.call-update) | async-done | bytes 1310736 | tf_op jit(solution)/shard_map/reduce_scatter | solution.py:254
  350.5 40.4 %reduce-scatter.22.cloned.1.call-done = bf16[320,2048]{1,0:T(8,128)(2,1)} async-done(((bf16[640,2048]{1,0:T(8,128)(2,1)}), bf16[320,2048]{1,0:T(8,128)(2,1)}) %reduce-scatter.22.cloned.1.call-update) | async-done | bytes 1310736 | tf_op jit(solution)/shard_map/reduce_scatter | solution.py:251
  390.9 40.5 %reduce-scatter.26.cloned.1.call-done = bf16[1024,640]{1,0:T(8,128)(2,1)} async-done(((bf16[2048,640]{1,0:T(8,128)(2,1)}), bf16[1024,640]{1,0:T(8,128)(2,1)}) %reduce-scatter.26.cloned.1.call-update) | async-done | bytes 1310736 | tf_op jit(solution)/shard_map/reduce_scatter | solution.py:257
  431.5 25.9 %reduce-scatter.14.cloned.1.call-done = bf16[320,1024]{1,0:T(8,128)(2,1)} async-done(((bf16[640,1024]{1,0:T(8,128)(2,1)}), bf16[320,1024]{1,0:T(8,128)(2,1)}) %reduce-scatter.14.cloned.1.call-update) | async-done | bytes 655376 | tf_op jit(solution)/shard_map/reduce_scatter | solution.py:239
  461.0 5.1 all-reduce.16
  466.5 34.3 %all-reduce.14 = (bf16[320]{0:T(512)(128)(2,1)S(1)}, bf16[128]{0:T(256)(128)(2,1)S(1)}, bf16[128]{0:T(256)(128)(2,1)S(1)}, bf16[320]{0:T(512)(128)(2,1)S(1)}, bf...) all-reduce(bf16[320]{0:T(512)(128)(2,1)S(1)} %dynamic-slice.5, ...), channel_id=1, replica_groups=mesh['rep'=4,'fsdp'=2,'seq'=4] {'rep','seq'}, use_global_device_ids=true, to_apply=%region_36.37 | all-reduce | flops 1536 | bytes 6144 | tf_op jit(solution)/shard_map/psum | solution.py:287
  504.2 2.0 fusion.61
  506.2 76.4 %all-reduce.20.cloned.1.call-done = (bf16[320,256]{1,0:T(8,128)(2,1)}, bf16[320,256]{1,0:T(8,128)(2,1)}, bf16[512,640]{1,0:T(8,128)(2,1)}, bf16[320,2048]{1,0:T(...) async-done(((bf16[320,256]{1,0:T(8,128)(2,1)}, bf16[320,256]{1,0:T(8,128)(2,1)}, bf16[512,640]{1,0:T(8,128)(2,1)}, bf16[320,2048]{1,0:T(8,128)(2,1)}, ...) | async-done | bytes 4915216 | tf_op jit(solution)/shard_map/psum | solution.py:281
  582.6 1.8 convert_element_type.261
  584.4 1.7 convert_element_type.263
  586.0 2.2 convert_element_type.265
  588.3 1.8 convert_element_type.267
  590.1 1.8 convert_element_type.269
  591.9 1.7 convert_element_type.271
  593.5 78.8 %all-gather.20.cloned.1.call-done = bf16[5120,1024]{1,0:T(8,128)(2,1)} async-done(((bf16[320,1024]{1,0:T(8,128)(2,1)}), bf16[5120,1024]{1,0:T(8,128)(2,1)}) %all-gather.20.cloned.1.call-update) | async-done | bytes 10485776 | tf_op jit(solution)/shard_map/all_gather | solution.py:86
  672.3 6.7 reduce_sum.233
  (291 shorter events, 41.7 us)
Async XLA Ops:
  7.2 55.9 %all-gather.10.cloned.1.call-start = ((), (), s32[]{:S(2)}) async-start(), calls=%async_computation.9 | async-start | bytes 1966080 | tf_op jit(solution)/shard_map/all_gather | solution.py:91
  7.9 69.5 %all-gather.12.cloned.1.call-start = ((), (), s32[]{:S(2)}) async-start(), calls=%async_computation.10 | async-start | bytes 1966080 | tf_op jit(solution)/shard_map/all_gather | solution.py:94
  8.7 11.9 %copy-start.73 = (u32[32]{0:T(128)S(1)}, u32[32]{0:T(128)}, u32[]{:S(2)}) copy-start(u32[32]{0:T(128)} %constant.78) | copy-start | bytes 388
  8.7 13.1 %copy-start.76 = (bf16[320]{0:T(512)(128)(2,1)S(1)}, bf16[320]{0:T(512)(128)(2,1)}, u32[]{:S(2)}) copy-start(bf16[320]{0:T(512)(128)(2,1)} %param.30) | copy-start | bytes 1924
  8.7 13.4 %copy-start.77 = (bf16[320]{0:T(512)(128)(2,1)S(1)}, bf16[320]{0:T(512)(128)(2,1)}, u32[]{:S(2)}) copy-start(bf16[320]{0:T(512)(128)(2,1)} %param.29) | copy-start | bytes 1924
  8.7 13.6 %copy-start.78 = (bf16[320]{0:T(512)(128)(2,1)S(1)}, bf16[320]{0:T(512)(128)(2,1)}, u32[]{:S(2)}) copy-start(bf16[320]{0:T(512)(128)(2,1)} %param.26) | copy-start | bytes 1924
  8.7 13.8 %copy-start.79 = (bf16[320]{0:T(512)(128)(2,1)S(1)}, bf16[320]{0:T(512)(128)(2,1)}, u32[]{:S(2)}) copy-start(bf16[320]{0:T(512)(128)(2,1)} %param.31) | copy-start | bytes 1924
  8.8 20.3 %copy-start.38 = (bf16[320,256]{1,0:T(8,128)(2,1)S(1)}, bf16[320,256]{1,0:T(8,128)(2,1)}, u32[]{:S(2)}) copy-start(bf16[320,256]{1,0:T(8,128)(2,1)} %param.20) | copy-start | bytes 491524
  8.8 98.1 %all-gather.14.cloned.1.call-start = ((), (), s32[]{:S(2)}) async-start(), calls=%async_computation.11 | async-start | bytes 3932160 | tf_op jit(solution)/shard_map/all_gather | solution.py:95
  9.5 30.0 %copy-start.39 = (bf16[320,256]{1,0:T(8,128)(2,1)S(1)}, bf16[320,256]{1,0:T(8,128)(2,1)}, u32[]{:S(2)}) copy-start(bf16[320,256]{1,0:T(8,128)(2,1)} %param.21) | copy-start | bytes 491524
  9.5 137.8 %all-gather.16.cloned.1.call-start = ((), (), s32[]{:S(2)}) async-start(), calls=%async_computation.12 | async-start | bytes 3932160 | tf_op jit(solution)/shard_map/all_gather | solution.py:96
  10.1 177.6 %all-gather.18.cloned.1.call-start = ((), (), s32[]{:S(2)}) async-start(), calls=%async_computation.13 | async-start | bytes 3932160 | tf_op jit(solution)/shard_map/all_gather | solution.py:97
  10.7 218.4 %reduce-scatter.12.cloned.1.call-start = ((), (), s32[]{:S(2)}) async-start(), calls=%async_computation.15 | async-start | bytes 655360 | tf_op jit(solution)/shard_map/reduce_scatter | solution.py:219
  10.8 43.3 %copy-start.74 = (f32[128]{0:T(128)}, f32[128]{0:T(128)S(1)}, u32[]{:S(2)}) copy-start(f32[128]{0:T(128)S(1)} %multiply_power_fusion) | copy-start | bytes 1540
  11.1 42.9 %copy-start.62 = (f32[256]{0:T(256)}, f32[256]{0:T(256)S(1)}, u32[]{:S(2)}) copy-start(f32[256]{0:T(256)S(1)} %fusion.45) | copy-start | bytes 3076
  11.1 54.1 %copy-start.48 = (f32[256]{0:T(256)}, f32[256]{0:T(256)S(1)}, u32[]{:S(2)}) copy-start(f32[256]{0:T(256)S(1)} %fusion.83) | copy-start | bytes 3076
  16.3 49.7 %copy-start.52 = (f32[2,1,128]{2,1,0:T(1,128)}, f32[2,1,128]{2,1,0:T(1,128)S(1)}, u32[]{:S(2)}) copy-start(f32[2,1,128]{2,1,0:T(1,128)S(1)} %convert_element_type.286) | copy-start | bytes 3076
  20.6 33.5 %copy-start.54 = (f32[2,1,128]{2,1,0:T(1,128)}, f32[2,1,128]{2,1,0:T(1,128)S(1)}, u32[]{:S(2)}) copy-start(f32[2,1,128]{2,1,0:T(1,128)S(1)} %convert_element_type.287) | copy-start | bytes 3076
  28.4 26.2 %copy-start.60 = (f32[256]{0:T(256)}, f32[256]{0:T(256)S(1)}, u32[]{:S(2)}) copy-start(f32[256]{0:T(256)S(1)} %dynamic-slice_convert_fusion) | copy-start | bytes 3076
  39.0 15.6 %copy-start.19 = (bf16[640,256]{1,0:T(8,128)(2,1)}, bf16[640,256]{1,0:T(8,128)(2,1)S(1)}, u32[]{:S(2)}) copy-start(bf16[640,256]{1,0:T(8,128)(2,1)S(1)} %all_gather.61) | copy-start | bytes 983044
  39.4 22.6 %copy-start.12 = (f32[256,256]{0,1:T(8,128)}, f32[256,256]{0,1:T(8,128)S(1)}, u32[]{:S(2)}) copy-start(f32[256,256]{0,1:T(8,128)S(1)} %get-tuple-element.71) | copy-start | bytes 786436
  39.4 22.6 %copy-start.71 = (f32[256]{0:T(256)}, f32[256]{0:T(256)S(1)}, u32[]{:S(2)}) copy-start(f32[256]{0:T(256)S(1)} %get-tuple-element.70) | copy-start | bytes 3076
  39.5 22.5 %copy-start.56 = (f32[256]{0:T(256)}, f32[256]{0:T(256)S(1)}, u32[]{:S(2)}) copy-start(f32[256]{0:T(256)S(1)} %fusion.84) | copy-start | bytes 3076
  54.7 11.5 %copy-start.25 = (f32[256,128]{0,1:T(8,128)}, f32[256,128]{0,1:T(8,128)S(1)}, u32[]{:S(2)}) copy-start(f32[256,128]{0,1:T(8,128)S(1)} %get-tuple-element.64) | copy-start | bytes 393220
  54.7 11.5 %copy-start.27 = (f32[256,128]{0,1:T(8,128)}, f32[256,128]{0,1:T(8,128)S(1)}, u32[]{:S(2)}) copy-start(f32[256,128]{0,1:T(8,128)S(1)} %get-tuple-element.65) | copy-start | bytes 393220
  207.2 46.6 %reduce-scatter.10.cloned.1.call-start = ((), (), s32[]{:S(2)}) async-start(), calls=%async_computation.14 | async-start | bytes 655360 | tf_op jit(solution)/shard_map/reduce_scatter | solution.py:216
  210.1 18.9 %copy-start.49 = (f32[256]{0:T(256)S(1)}, f32[256]{0:T(256)}, u32[]{:S(2)}) copy-start(f32[256]{0:T(256)} %copy-done.48) | copy-start | bytes 3076
  222.5 32.2 %copy-start.61 = (f32[256]{0:T(256)S(1)}, f32[256]{0:T(256)}, u32[]{:S(2)}) copy-start(f32[256]{0:T(256)} %copy-done.60) | copy-start | bytes 3076
  222.5 32.3 %copy-start.75 = (f32[128]{0:T(128)S(1)}, f32[128]{0:T(128)}, u32[]{:S(2)}) copy-start(f32[128]{0:T(128)} %copy-done.74) | copy-start | bytes 1540
  222.5 32.8 %copy-start.13 = (f32[256,256]{0,1:T(8,128)S(1)}, f32[256,256]{0,1:T(8,128)}, u32[]{:S(2)}) copy-start(f32[256,256]{0,1:T(8,128)} %copy-done.12) | copy-start | bytes 786436
  222.5 32.8 %copy-start.55 = (f32[2,1,128]{2,1,0:T(1,128)S(1)}, f32[2,1,128]{2,1,0:T(1,128)}, u32[]{:S(2)}) copy-start(f32[2,1,128]{2,1,0:T(1,128)} %copy-done.54) | copy-start | bytes 3076
  222.5 32.8 %copy-start.57 = (f32[256]{0:T(256)S(1)}, f32[256]{0:T(256)}, u32[]{:S(2)}) copy-start(f32[256]{0:T(256)} %copy-done.56) | copy-start | bytes 3076
  222.5 33.0 %copy-start.72 = (f32[256]{0:T(256)S(1)}, f32[256]{0:T(256)}, u32[]{:S(2)}) copy-start(f32[256]{0:T(256)} %copy-done.71) | copy-start | bytes 3076
  222.6 61.3 %reduce-scatter.18.cloned.1.call-start = ((), (), s32[]{:S(2)}) async-start(), calls=%async_computation.18 | async-start | bytes 491520 | tf_op jit(solution)/shard_map/reduce_scatter | solution.py:245
  231.2 52.8 %reduce-scatter.16.cloned.1.call-start = ((), (), s32[]{:S(2)}) async-start(), calls=%async_computation.17 | async-start | bytes 491520 | tf_op jit(solution)/shard_map/reduce_scatter | solution.py:242
  256.8 53.1 %reduce-scatter.20.cloned.1.call-start = ((), (), s32[]{:S(2)}) async-start(), calls=%async_computation.19 | async-start | bytes 1966080 | tf_op jit(solution)/shard_map/reduce_scatter | solution.py:248
  259.6 90.9 %reduce-scatter.24.cloned.1.call-start = ((), (), s32[]{:S(2)}) async-start(), calls=%async_computation.21 | async-start | bytes 3932160 | tf_op jit(solution)/shard_map/reduce_scatter | solution.py:254
  262.1 128.8 %reduce-scatter.22.cloned.1.call-start = ((), (), s32[]{:S(2)}) async-start(), calls=%async_computation.20 | async-start | bytes 3932160 | tf_op jit(solution)/shard_map/reduce_scatter | solution.py:251
  265.7 165.7 %reduce-scatter.26.cloned.1.call-start = ((), (), s32[]{:S(2)}) async-start(), calls=%async_computation.22 | async-start | bytes 3932160 | tf_op jit(solution)/shard_map/reduce_scatter | solution.py:257
  269.6 187.8 %reduce-scatter.14.cloned.1.call-start = ((), (), s32[]{:S(2)}) async-start(), calls=%async_computation.16 | async-start | bytes 1966080 | tf_op jit(solution)/shard_map/reduce_scatter | solution.py:239
  283.8 298.8 %all-reduce.20.cloned.1.call-start = ((), (), s32[]{:S(2)}) async-start(), calls=%async_computation.24 | async-start | bytes 9830400 | tf_op jit(solution)/shard_map/psum | solution.py:281
  431.4 27.3 %copy-start.20 = (bf16[640,256]{1,0:T(8,128)(2,1)S(1)}, bf16[640,256]{1,0:T(8,128)(2,1)}, u32[]{:S(2)}) copy-start(bf16[640,256]{1,0:T(8,128)(2,1)} %copy-done.19) | copy-start | bytes 983044
  431.4 27.6 %copy-start.22 = (bf16[640,256]{1,0:T(8,128)(2,1)S(1)}, bf16[640,256]{1,0:T(8,128)(2,1)}, u32[]{:S(2)}) copy-start(bf16[640,256]{1,0:T(8,128)(2,1)} %copy-done.21) | copy-start | bytes 983044
  431.4 27.6 %copy-start.40 = (bf16[256,256]{1,0:T(8,128)(2,1)S(1)}, bf16[256,256]{1,0:T(8,128)(2,1)}, u32[]{:S(2)}) copy-start(bf16[256,256]{1,0:T(8,128)(2,1)} %reduce-scatter.12.cloned.1.call-done) | copy-start | bytes 393220
  431.4 27.9 %copy-start.4 = (bf16[640,1024]{1,0:T(8,128)(2,1)S(1)}, bf16[640,1024]{1,0:T(8,128)(2,1)}, u32[]{:S(2)}) copy-start(bf16[640,1024]{1,0:T(8,128)(2,1)} %all-gather.10.cloned.1.call-done) | copy-start | bytes 3932164
  431.4 240.9 %all-gather.20.cloned.1.call-start = ((), (), s32[]{:S(2)}) async-start(), calls=%async_computation.23 | async-start | bytes 11141120 | tf_op jit(solution)/shard_map/all_gather | solution.py:86
  459.4 44.7 %copy-start.63 = (f32[256]{0:T(256)S(1)}, f32[256]{0:T(256)}, u32[]{:S(2)}) copy-start(f32[256]{0:T(256)} %copy-done.62) | copy-start | bytes 3076
  459.4 44.8 %copy-start.3 = (f32[256,640]{1,0:T(8,128)S(1)}, f32[256,640]{1,0:T(8,128)}, u32[]{:S(2)}) copy-start(f32[256,640]{1,0:T(8,128)} %copy-done.2) | copy-start | bytes 1966084
  (53 other events, 139.3 us)
Sparse Core Ops, SparseCore 0:
  9.5 31.1 all-gather.9
  42.2 24.0 all-gather.11
  67.8 38.9 all-gather.13
  108.3 38.9 all-gather.15
  148.7 38.9 all-gather.17
  207.4 21.6 reduce-scatter.11
  232.1 21.6 reduce-scatter.9
  256.1 12.4 reduce-scatter.17
  271.4 12.5 reduce-scatter.15
  286.7 23.2 reduce-scatter.19
  312.8 37.6 reduce-scatter.23
  353.2 37.6 reduce-scatter.21
  393.7 37.6 reduce-scatter.25
  434.1 23.2 reduce-scatter.13
  461.7 120.8 all-reduce.19
  584.7 87.5 all-gather.19
